TPU v7x, 128 devices: a whole 4x4x4 slice. The times are simulated.
128 devices in a mesh: req: 16 (over y, z), mlp: 8 (over x, core).
Axes of the slice: x: 4, y: 4, z: 4, core: 2. Of those that a mesh axis runs over, the one named last changes fastest.
Arguments:
- blocks: bfloat16 [2048, 4096], P('req'), may hold values from -6 to 6
- token_embed: bfloat16 [2048, 4096], P('req'), may hold values from -6 to 6
- accepted: int32 [2048], P('req'), may hold values 0 or 1
- prompt_len: int32 [16], P('req'), may hold values from 2 to 512, as said below
- cache_len: int32 [16, 8], P('req'), may hold values from 1 to 1024, as said below
- prompt_kv: bfloat16 [16, 512, 2048], P('req', None, 'mlp'), may hold values from -364 to 364
- cache_kv: bfloat16 [16, 8, 1024, 2048], P('req', None, None, 'mlp'), may hold values from -6 to 6
- attn_gain: float32 [4096], replicated, may hold values from 0.25 to 1.75
- w_q: bfloat16 [4096, 4096], P(None, 'mlp'), may hold values from -0.09375 to 0.09375
- w_kv: bfloat16 [4096, 2048], P(None, 'mlp'), may hold values from -0.09375 to 0.09375
- w_o: bfloat16 [4096, 4096], P('mlp'), may hold values from -0.09375 to 0.09375
- mlp_gain: float32 [4096], replicated, may hold values from 0.25 to 1.75
- w_gate: bfloat16 [4096, 7168], P('req', 'mlp'), may hold values from -0.09375 to 0.09375
- w_up: bfloat16 [4096, 7168], P('req', 'mlp'), may hold values from -0.09375 to 0.09375
- w_down: bfloat16 [7168, 4096], P('mlp'), may hold values from -0.0625 to 0.0625
Outputs:
- denoised: bfloat16 [2048, 4096], P('req')
Inputs may be any that keep to these rules, and one draw needn't show every extreme that they name: `prompt_len`: shared by the 8 requests of a group; some group has a prompt of exactly 512. `cache_len`: every group has a request with exactly 1024 cached tokens.
All inputs are finite; a program needn't handle non-finite values. No bound on the sum of `accepted` on one device may be relied on, other than what follows from the above.
Results may differ from a plain program's by a relative error of at most 0.022.
Values may be sent and summed in bfloat16 or wider, within the bound.
A program may use at most 128 MiB of HBM per device.

v0:
```python
import math
import jax
import jax.numpy as jnp
from jax import lax
from jax.sharding import PartitionSpec as P

HEAD_DIM = 128
REQS = 8
BLOCK = 16
EPSILON = 1e-05
THETA = 500000.0


def rms_scale(stream, gain):
    widened = stream.astype(jnp.float32)
    mean_square = jnp.mean(widened * widened, axis=-1, keepdims=True)
    return (widened * lax.rsqrt(mean_square + EPSILON) * gain).astype(jnp.bfloat16)


def rope(values, positions):
    head_size = values.shape[-1]
    half_size = head_size // 2
    frequency = THETA ** (-2.0 * jnp.arange(half_size, dtype=jnp.float32) / head_size)
    angles = positions.astype(jnp.float32)[:, None] * frequency[None, :]
    cosine = jnp.cos(angles)[:, None, :]
    sine = jnp.sin(angles)[:, None, :]
    first = values[..., :half_size]
    second = values[..., half_size:]
    return jnp.concatenate(
        [first * cosine - second * sine, second * cosine + first * sine], axis=-1
    )


def attend_one(
    queries, block_keys, block_values, prompt_part, cached_part, prompt_size, cache_size
):
    block_len, head_count, head_size = queries.shape
    kv_heads = block_keys.shape[1]
    group_size = head_count // kv_heads
    grouped = queries.reshape(block_len, kv_heads, group_size, head_size)
    scale = 1.0 / math.sqrt(head_size)

    def scores(keys):
        return (
            jnp.einsum("tkgd,lkd->kgtl", grouped, keys, preferred_element_type=jnp.float32) * scale
        )

    prompt_score = scores(prompt_part[:, :, 0])
    cache_score = scores(cached_part[:, :, 0])
    block_score = scores(block_keys)
    prompt_ok = jnp.arange(prompt_part.shape[0], dtype=jnp.int32) < prompt_size
    cache_ok = jnp.arange(cached_part.shape[0], dtype=jnp.int32) < cache_size
    prompt_score = jnp.where(prompt_ok, prompt_score, -1e30)
    cache_score = jnp.where(cache_ok, cache_score, -1e30)
    largest = jnp.maximum(
        jnp.maximum(
            jnp.max(prompt_score, -1, keepdims=True), jnp.max(cache_score, -1, keepdims=True)
        ),
        jnp.max(block_score, -1, keepdims=True),
    )
    prompt_exp = jnp.exp(prompt_score - largest)
    cache_exp = jnp.exp(cache_score - largest)
    block_exp = jnp.exp(block_score - largest)
    total = (
        jnp.sum(prompt_exp, -1, keepdims=True)
        + jnp.sum(cache_exp, -1, keepdims=True)
        + jnp.sum(block_exp, -1, keepdims=True)
    )
    prompt_w = (prompt_exp / total).astype(jnp.bfloat16)
    cache_w = (cache_exp / total).astype(jnp.bfloat16)
    block_w = (block_exp / total).astype(jnp.bfloat16)
    result = jnp.einsum(
        "kgtl,lkd->tkgd", prompt_w, prompt_part[:, :, 1], preferred_element_type=jnp.float32
    )
    result = result + jnp.einsum(
        "kgtl,lkd->tkgd", cache_w, cached_part[:, :, 1], preferred_element_type=jnp.float32
    )
    result = result + jnp.einsum(
        "kgtl,lkd->tkgd", block_w, block_values, preferred_element_type=jnp.float32
    )
    return result.reshape(block_len, head_count * head_size).astype(jnp.bfloat16)


def swiglu(gate, up_part):
    return (jax.nn.silu(gate) * up_part).astype(jnp.bfloat16)


def body(
    blocks,
    token_embed,
    accepted,
    prompt_len,
    cache_len,
    prompt_kv,
    cache_kv,
    attn_gain,
    w_q,
    w_kv,
    w_o,
    mlp_gain,
    w_gate,
    w_up,
    w_down,
):
    row_count = blocks.shape[0]
    prompt_size = prompt_len[0]
    cache_sizes = cache_len[0]
    positions = (
        prompt_size + cache_sizes[:, None] + jnp.arange(BLOCK, dtype=jnp.int32)[None, :]
    ).reshape(-1)
    local_kv = w_kv.shape[1] // (2 * HEAD_DIM)
    local_heads = w_q.shape[1] // HEAD_DIM
    prompt_part = prompt_kv[0].reshape(-1, local_kv, 2, HEAD_DIM)
    cached = cache_kv[0].reshape(REQS, -1, local_kv, 2, HEAD_DIM)

    def one_pass(stream):
        normed = rms_scale(stream, attn_gain)
        queries = rope(
            jnp.dot(normed, w_q, preferred_element_type=jnp.float32).reshape(
                row_count, local_heads, HEAD_DIM
            ),
            positions,
        ).astype(jnp.bfloat16)
        key_value = jnp.dot(normed, w_kv, preferred_element_type=jnp.float32).reshape(
            row_count, local_kv, 2, HEAD_DIM
        )
        keys = rope(key_value[:, :, 0], positions).astype(jnp.bfloat16)
        values = key_value[:, :, 1].astype(jnp.bfloat16)

        def attend_request(items):
            query_part, key_part, value_part, cache_part, cache_size = items
            return attend_one(
                query_part, key_part, value_part, prompt_part, cache_part, prompt_size, cache_size
            )

        attended = lax.map(
            attend_request,
            (
                queries.reshape(REQS, BLOCK, local_heads, HEAD_DIM),
                keys.reshape(REQS, BLOCK, local_kv, HEAD_DIM),
                values.reshape(REQS, BLOCK, local_kv, HEAD_DIM),
                cached,
                cache_sizes,
            ),
        )
        attended = attended.reshape(row_count, local_heads * HEAD_DIM)
        mixed = lax.psum(jnp.dot(attended, w_o, preferred_element_type=jnp.float32), "mlp")
        after_attn = (stream.astype(jnp.float32) + mixed).astype(jnp.bfloat16)
        normed2 = rms_scale(after_attn, mlp_gain)
        pass_gate, pass_up = (
            lax.all_gather(w_gate, "req", axis=0, tiled=True),
            lax.all_gather(w_up, "req", axis=0, tiled=True),
        )
        gate = jnp.dot(normed2, pass_gate, preferred_element_type=jnp.float32)
        up_part = jnp.dot(normed2, pass_up, preferred_element_type=jnp.float32)
        hidden = swiglu(gate, up_part)
        down = lax.psum(jnp.dot(hidden, w_down, preferred_element_type=jnp.float32), "mlp")
        return (after_attn.astype(jnp.float32) + down).astype(jnp.bfloat16)

    first = one_pass(blocks)
    second_input = jnp.where(accepted[:, None] == 1, token_embed, first)
    return one_pass(second_input)


def solution(mesh):
    return jax.shard_map(
        body,
        mesh=mesh,
        in_specs=(
            P("req", None),
            P("req", None),
            P("req"),
            P("req"),
            P("req", None),
            P("req", None, "mlp"),
            P("req", None, None, "mlp"),
            P(),
            P(None, "mlp"),
            P(None, "mlp"),
            P("mlp", None),
            P(),
            P("req", "mlp"),
            P("req", "mlp"),
            P("mlp", None),
        ),
        out_specs=P("req", None),
        check_vma=False,
    )
```

profile of v0, /device:TPU:0, one launch (start us, length us, event | category | flops | bytes accessed | tf_op | source)
XLA Modules:
  0.0 504.8 jit_solution(11946350769607813790)
XLA Ops:
  7.4 1.7 fusion.76
  9.3 1.8 fusion.119
  12.8 2.9 fusion.121
  17.3 1.4 copy.63
  18.8 6.4 %copy.26 = bf16[1,8,1024,256]{2,3,1,0:T(8,128)(2,1)} copy(bf16[1,8,1024,256]{3,2,1,0:T(8,128)(2,1)} %param.25) | data formatting | bytes 8388608 | tf_op args[6]
  25.2 6.5 %copy.30 = bf16[8,1024,1,2,128]{4,1,3,2,0:T(8,128)(2,1)} copy(bf16[8,1024,1,2,128]{1,4,3,0,2:T(8,128)(2,1)} %bitcast.294) | data formatting | bytes 8388608 | tf_op jit(solution)/shard_map/while | solution.py:136
  33.1 45.7 %while.20 = (s32[]{:T(128)}, bf16[8,16,512]{2,1,0:T(8,128)(2,1)S(1)}, s32[]{:T(128)}, bf16[8,16,4,128]{3,1,0,2:T(8,128)(2,1)S(1)}, bf16[512,1,2,128]{3,0,2,1:T(8...) while((s32[]{:T(128)}, ...), condition=%wide.region_8.9_spmd, body=%wide.region_1.8_spmd.sunk | while | flops 51675520 | bytes 3347849 | solution.py:136
  78.8 4.2 fusion.154
  84.3 68.4 %all-reduce.5.cloned.1.call-done = f32[128,4096]{1,0:T(8,128)} async-done(((f32[128,4096]{1,0:T(8,128)}), f32[128,4096]{1,0:T(8,128)}) %all-reduce.5.cloned.1.call-update) | async-done | bytes 2097168 | tf_op jit(solution)/shard_map/psum | solution.py:147
  152.7 2.3 fusion.80
  155.5 5.2 %fusion.117 = f32[128,896]{1,0:T(8,128)} fusion(bf16[4096,896]{1,0:T(8,128)(2,1)} %all-gather.3.cloned.1.call-done, bf16[128,4096]{1,0:T(8,128)(2,1)S(1)} %get-tuple-element.160, f32[4096]{0:T(1024)S(1)} %copy-done.6, f32[128]{0:T(128)} %add_rsqrt_fusion.2), kind=kOutput, calls=%fused_computation.162 | convolution fusion | flops 941621248 | bytes 8864256 | tf_op jit(solution)/shard_map/dot_general | solution.py:154
  160.7 61.8 %all-gather.5.cloned.1.call-done = bf16[4096,896]{1,0:T(8,128)(2,1)} async-done(((bf16[256,896]{1,0:T(8,128)(2,1)}), bf16[4096,896]{1,0:T(8,128)(2,1)}) %all-gather.5.cloned.1.call-update) | async-done | bytes 7340048 | tf_op jit(solution)/shard_map/all_gather | solution.py:152
  222.5 9.0 %fusion.96 = f32[128,4096]{1,0:T(8,128)} fusion(bf16[896,4096]{1,0:T(8,128)(2,1)} %param.33, bf16[4096,896]{1,0:T(8,128)(2,1)} %all-gather.5.cloned.1.call-done, f32[128,896]{1,0:T(8,128)} %fusion.117, bf16[128,4096]{1,0:T(8,128)(2,1)S(1)} %get-tuple-element.160, f32[4096]{0:T(1024)S(1)} %copy-done.6, f32[128]{0:T(128)} %add_rsqrt_fusion.2), kind=kOutput, calls=%fused_computation.148 | convolution fusion | flops 1881833472 | bytes 18301440 | tf_op jit(solution)/shard_map/dot_general | solution.py:157
  233.0 63.9 %all-reduce.7.cloned.1.call-done = f32[128,4096]{1,0:T(8,128)} async-done(((f32[128,4096]{1,0:T(8,128)}), f32[128,4096]{1,0:T(8,128)}) %all-reduce.7.cloned.1.call-update) | async-done | bytes 2097168 | tf_op jit(solution)/shard_map/psum | solution.py:157
  296.9 2.5 fusion.84
  301.1 3.3 fusion.113
  305.4 39.2 %while.21 = (s32[]{:T(128)}, bf16[8,16,512]{2,1,0:T(8,128)(2,1)S(1)}, s32[]{:T(128)}, bf16[8,16,4,128]{3,1,0,2:T(8,128)(2,1)S(1)}, bf16[512,1,2,128]{3,0,2,1:T(8...) while((s32[]{:T(128)}, ...), condition=%wide.region_20.21_spmd, body=%wide.region_13.20_spmd.sunk | while | flops 51675520 | bytes 3379597 | solution.py:136
  344.6 4.3 fusion.155
  348.9 65.2 %all-reduce.9.cloned.1.call-done = f32[128,4096]{1,0:T(8,128)} async-done(((f32[128,4096]{1,0:T(8,128)}), f32[128,4096]{1,0:T(8,128)}) %all-reduce.9.cloned.1.call-update) | async-done | bytes 2097168 | tf_op jit(solution)/shard_map/psum | solution.py:147
  414.2 2.0 fusion.88
  416.2 4.4 fusion.109
  420.6 9.0 %fusion.95 = f32[128,4096]{1,0:T(8,128)} fusion(bf16[896,4096]{1,0:T(8,128)(2,1)} %param.33, bf16[4096,896]{1,0:T(8,128)(2,1)} %all-gather.5.cloned.1.call-done, f32[128,896]{1,0:T(8,128)S(1)} %fusion.109, bf16[128,4096]{1,0:T(8,128)(2,1)S(1)} %get-tuple-element.156, f32[128]{0:T(128)S(1)} %add_rsqrt_fusion, f32[4096]{0:T(1024)S(1)} %copy-done.6), kind=kOutput, calls=%fused_computation.147 | convolution fusion | flops 1881833472 | bytes 18301440 | tf_op jit(solution)/shard_map/dot_general | solution.py:157
  429.6 65.3 %all-reduce.11.cloned.1.call-done = f32[128,4096]{1,0:T(8,128)} async-done(((f32[128,4096]{1,0:T(8,128)}), f32[128,4096]{1,0:T(8,128)}) %all-reduce.11.cloned.1.call-update) | async-done | bytes 2097168 | tf_op jit(solution)/shard_map/psum | solution.py:157
  494.9 2.8 fusion.91
  (368 shorter events, 93.6 us)
Async XLA Ops:
  7.4 1.9 copy-start
  7.4 145.3 %all-reduce.5.cloned.1.call-start = ((), (), s32[]{:S(2)}) async-start(), calls=%async_computation | async-start | bytes 4194304 | tf_op jit(solution)/shard_map/psum | solution.py:147
  7.4 9.0 %copy-start.9 = (f32[64]{0:T(128)}, f32[64]{0:T(128)S(1)}, u32[]{:S(2)}) copy-start(f32[64]{0:T(128)S(1)} %multiply_power_fusion) | copy-start | bytes 772
  9.3 3.3 copy-start.14
  9.3 3.5 copy-start.2
  9.3 3.5 copy-start.11
  12.8 3.6 copy-start.7
  25.2 6.5 %copy-start.5 = (bf16[1,512,256]{2,1,0:T(8,128)(2,1)S(1)}, bf16[1,512,256]{2,1,0:T(8,128)(2,1)}, u32[]{:S(2)}) copy-start(bf16[1,512,256]{2,1,0:T(8,128)(2,1)} %param.24) | copy-start | bytes 786436
  83.0 72.5 %all-gather.3.cloned.1.call-start = ((), (), s32[]{:S(2)}) async-start(), calls=%async_computation.1 | async-start | bytes 7798784 | tf_op jit(solution)/shard_map/all_gather | solution.py:151
  83.6 138.9 %all-gather.5.cloned.1.call-start = ((), (), s32[]{:S(2)}) async-start(), calls=%async_computation.2 | async-start | bytes 7798784 | tf_op jit(solution)/shard_map/all_gather | solution.py:152
  84.2 71.3 %copy-start.6 = (f32[4096]{0:T(1024)S(1)}, f32[4096]{0:T(1024)}, u32[]{:S(2)}) copy-start(f32[4096]{0:T(1024)} %param.30) | copy-start | bytes 49156
  84.2 212.6 %all-reduce.7.cloned.1.call-start = ((), (), s32[]{:S(2)}) async-start(), calls=%async_computation.3 | async-start | bytes 4194304 | tf_op jit(solution)/shard_map/psum | solution.py:157
  231.5 182.6 %all-reduce.9.cloned.1.call-start = ((), (), s32[]{:S(2)}) async-start(), calls=%async_computation.4 | async-start | bytes 4194304 | tf_op jit(solution)/shard_map/psum | solution.py:147
  296.9 3.5 copy-start.12
  299.4 1.0 copy-start.3
  300.3 0.7 copy-start.13
  301.1 3.3 copy-start.8
  301.1 3.3 copy-start.10
  304.4 1.0 copy-start.15
  348.8 65.3 %copy-start.4 = (bf16[128,4096]{1,0:T(8,128)(2,1)S(1)}, bf16[128,4096]{1,0:T(8,128)(2,1)}, u32[]{:S(2)}) copy-start(bf16[128,4096]{1,0:T(8,128)(2,1)} %copy-done.3) | copy-start | bytes 3145732
  348.9 146.0 %all-reduce.11.cloned.1.call-start = ((), (), s32[]{:S(2)}) async-start(), calls=%async_computation.5 | async-start | bytes 4194304 | tf_op jit(solution)/shard_map/psum | solution.py:157
  429.6 68.0 %copy-start.1 = (bf16[4096,256]{1,0:T(8,128)(2,1)S(1)}, bf16[4096,256]{1,0:T(8,128)(2,1)}, u32[]{:S(2)}) copy-start(bf16[4096,256]{1,0:T(8,128)(2,1)} %param.28) | copy-start | bytes 6291460
Sparse Core Ops, SparseCore 0:
  83.2 69.5 all-reduce.4
  231.7 65.1 all-reduce.6
  349.0 65.1 all-reduce.8
  429.7 65.1 all-reduce.10
Sparse Core Ops, SparseCore 1:
  85.7 68.7 all-gather.2
  156.6 65.9 all-gather.4
where the time goes:
time: 507 us; the launch traced here: 505 us
  waiting for transfers between devices  326 us (64%)
  matrix products  72.5 us (14%)
  local copies, waits for them, and re-layouts  45.8 us (9%)
  other arithmetic  43.5 us (9%)
  between operations  15.6 us (3%)
    psum x2, waiting for transfers between devices, one_pass(): lax.psum(jnp.dot(attended, w_o, preferred_element_type=jnp.float32), 'mlp')  134 us
    psum x2, waiting for transfers between devices, one_pass(): lax.psum(jnp.dot(hidden, w_down, preferred_element_type=jnp.float32), 'mlp')  129 us
    all_gather x1, waiting for transfers between devices, one_pass(): lax.all_gather(w_up, 'req', axis=0, tiled=True)  61.8 us
    dot_general x2, matrix products, one_pass(): jnp.dot(hidden, w_down, preferred_element_type=jnp.float32)  18 us
    squeeze x16, local copies, waits for them, and re-layouts, one_pass(): lax.map(attend_request, (queries.reshape(REQS, BLOCK, local_heads, HEAD_D...  17.3 us
    dot_general x48, matrix products, scores(): jnp.einsum('tkgd,lkd->kgtl', grouped, keys, preferred_element_type=jnp.fl...  11.7 us
    lt x16, other arithmetic, attend_one(): prompt_ok = jnp.arange(prompt_part.shape[0], dtype=jnp.int32) < prompt_size  10.5 us
    lt x16, other arithmetic, attend_one(): cache_ok = jnp.arange(cached_part.shape[0], dtype=jnp.int32) < cache_size  10.4 us
  transfers between devices with their start and end apart: 6, of which 5 were waited for; matrix products, arithmetic and copies ran while one was open for 2% of the time, Pallas kernels for 0%

commit v1 on v0

--- a/solution.py
+++ b/solution.py
@@ -154,7 +154,10 @@
         gate = jnp.dot(normed2, pass_gate, preferred_element_type=jnp.float32)
         up_part = jnp.dot(normed2, pass_up, preferred_element_type=jnp.float32)
         hidden = swiglu(gate, up_part)
-        down = lax.psum(jnp.dot(hidden, w_down, preferred_element_type=jnp.float32), "mlp")
+        down = jnp.sum(
+            lax.all_gather(jnp.dot(hidden, w_down, preferred_element_type=jnp.float32), "mlp"),
+            axis=0,
+        )
         return (after_attn.astype(jnp.float32) + down).astype(jnp.bfloat16)
 
     first = one_pass(blocks)

time: 507 us -> 563 us (1.11)
  waiting for transfers between devices: 326 us -> 366 us
  other arithmetic: 43.5 us -> 59.9 us
    all_gather x0 -> x2, waiting for transfers between devices: none -> 168 us  [one_pass(): lax.all_gather(jnp.dot(hidden, w_down, preferred_element_type=jnp.float32...]
    psum x2 -> x0, waiting for transfers between devices: 129 us -> none  [one_pass(): lax.psum(jnp.dot(hidden, w_down, preferred_element_type=jnp.float32), 'mlp')]
    reduce_sum x0 -> x2, other arithmetic: none -> 17.6 us  [one_pass(): jnp.sum(lax.all_gather(jnp.dot(hidden, w_down, preferred_element_type=jnp...]
where the time goes in v1:
time: 563 us; the launch traced here: 560 us
  waiting for transfers between devices  366 us (65%)
  matrix products  72.5 us (13%)
  other arithmetic  59.9 us (11%)
  local copies, waits for them, and re-layouts  45 us (8%)
  between operations  15.6 us (3%)
    all_gather x2, waiting for transfers between devices, one_pass(): lax.all_gather(jnp.dot(hidden, w_down, preferred_element_type=jnp.float32...  168 us
    psum x2, waiting for transfers between devices, one_pass(): lax.psum(jnp.dot(attended, w_o, preferred_element_type=jnp.float32), 'mlp')  135 us
    all_gather x1, waiting for transfers between devices, one_pass(): lax.all_gather(w_up, 'req', axis=0, tiled=True)  61.7 us
    dot_general x2, matrix products, one_pass(): jnp.dot(hidden, w_down, preferred_element_type=jnp.float32)  18.1 us
    reduce_sum x2, other arithmetic, one_pass(): jnp.sum(lax.all_gather(jnp.dot(hidden, w_down, preferred_element_type=jnp...  17.6 us
    squeeze x16, local copies, waits for them, and re-layouts, one_pass(): lax.map(attend_request, (queries.reshape(REQS, BLOCK, local_heads, HEAD_D...  17.3 us
    dot_general x48, matrix products, scores(): jnp.einsum('tkgd,lkd->kgtl', grouped, keys, preferred_element_type=jnp.fl...  11.7 us
  transfers between devices with their start and end apart: 6, of which 5 were waited for; matrix products, arithmetic and copies ran while one was open for 2% of the time, Pallas kernels for 0%

profile of v1, /device:TPU:0, one launch (start us, length us, event | category | flops | bytes accessed | tf_op | source)
XLA Modules:
  0.0 560.1 jit_solution(5331567460607469576)
XLA Ops:
  9.3 1.8 fusion.119
  12.8 2.9 fusion.121
  18.8 6.4 %copy.26 = bf16[1,8,1024,256]{2,3,1,0:T(8,128)(2,1)} copy(bf16[1,8,1024,256]{3,2,1,0:T(8,128)(2,1)} %param.25) | data formatting | bytes 8388608 | tf_op args[6]
  25.2 6.5 %copy.30 = bf16[8,1024,1,2,128]{4,1,3,2,0:T(8,128)(2,1)} copy(bf16[8,1024,1,2,128]{1,4,3,0,2:T(8,128)(2,1)} %bitcast.298) | data formatting | bytes 8388608 | tf_op jit(solution)/shard_map/while | solution.py:136
  33.1 44.1 %while.20 = (s32[]{:T(128)}, bf16[8,16,512]{2,1,0:T(8,128)(2,1)S(1)}, s32[]{:T(128)}, bf16[8,16,4,128]{3,1,0,2:T(8,128)(2,1)S(1)}, bf16[512,1,2,128]{3,0,2,1:T(8...) while((s32[]{:T(128)}, ...), condition=%wide.region_8.9_spmd, body=%wide.region_1.8_spmd.sunk | while | flops 51675520 | bytes 3347849 | solution.py:136
  77.2 4.2 fusion.154
  82.7 68.5 %all-reduce.3.cloned.1.call-done = f32[128,4096]{1,0:T(8,128)} async-done(((f32[128,4096]{1,0:T(8,128)}), f32[128,4096]{1,0:T(8,128)}) %all-reduce.3.cloned.1.call-update) | async-done | bytes 2097168 | tf_op jit(solution)/shard_map/psum | solution.py:147
  151.2 2.3 fusion.80
  154.0 5.2 fusion.117
  159.2 61.7 %all-gather.9.cloned.1.call-done = bf16[4096,896]{1,0:T(8,128)(2,1)} async-done(((bf16[256,896]{1,0:T(8,128)(2,1)}), bf16[4096,896]{1,0:T(8,128)(2,1)}) %all-gather.9.cloned.1.call-update) | async-done | bytes 7340048 | tf_op jit(solution)/shard_map/all_gather | solution.py:152
  220.9 9.1 %fusion.96 = f32[128,4096]{1,0:T(8,128)} fusion(bf16[896,4096]{1,0:T(8,128)(2,1)} %param.33, bf16[4096,896]{1,0:T(8,128)(2,1)} %all-gather.9.cloned.1.call-done, f32[128,896]{1,0:T(8,128)} %fusion.117, bf16[128,4096]{1,0:T(8,128)(2,1)S(1)} %get-tuple-element.160, f32[4096]{0:T(1024)S(1)} %copy-done.6, f32[128]{0:T(128)} %add_rsqrt_fusion.2), kind=kOutput, calls=%fused_computation.148 | convolution fusion | flops 1881833472 | bytes 18301440 | tf_op jit(solution)/shard_map/dot_general | solution.py:158
  231.5 83.2 %all-gather.11.cloned.1.call-done = f32[1024,4096]{1,0:T(8,128)} async-done(((f32[128,4096]{1,0:T(8,128)}), f32[1024,4096]{1,0:T(8,128)}) %all-gather.11.cloned.1.call-update) | async-done | bytes 16777232 | tf_op jit(solution)/shard_map/all_gather | solution.py:158
  314.7 8.7 %reduce_sum.110 = f32[128,4096]{1,0:T(8,128)} reduce(f32[8,128,4096]{2,1,0:T(8,128)} %bitcast.296, f32[]{:T(128)} %constant.65.clone.1), dimensions={0}, to_apply=%region_11.12 | reduce | flops 3670016 | bytes 18874372 | tf_op jit(solution)/shard_map/reduce_sum | solution.py:157
  323.5 2.5 fusion.84
  327.7 3.3 fusion.113
  332.0 38.7 %while.21 = (s32[]{:T(128)}, bf16[8,16,512]{2,1,0:T(8,128)(2,1)S(1)}, s32[]{:T(128)}, bf16[8,16,4,128]{3,1,0,2:T(8,128)(2,1)S(1)}, bf16[512,1,2,128]{3,0,2,1:T(8...) while((s32[]{:T(128)}, ...), condition=%wide.region_20.21_spmd, body=%wide.region_13.20_spmd.sunk | while | flops 51675520 | bytes 3379597 | solution.py:136
  370.7 4.2 fusion.155
  375.0 66.3 %all-reduce.5.cloned.1.call-done = f32[128,4096]{1,0:T(8,128)} async-done(((f32[128,4096]{1,0:T(8,128)}), f32[128,4096]{1,0:T(8,128)}) %all-reduce.5.cloned.1.call-update) | async-done | bytes 2097168 | tf_op jit(solution)/shard_map/psum | solution.py:147
  441.3 2.0 fusion.88
  443.3 4.4 fusion.109
  447.7 9.0 %fusion.95 = f32[128,4096]{1,0:T(8,128)} fusion(bf16[896,4096]{1,0:T(8,128)(2,1)} %param.33, bf16[4096,896]{1,0:T(8,128)(2,1)} %all-gather.9.cloned.1.call-done, f32[128,896]{1,0:T(8,128)S(1)} %fusion.109, bf16[128,4096]{1,0:T(8,128)(2,1)S(1)} %get-tuple-element.156, f32[128]{0:T(128)S(1)} %add_rsqrt_fusion, f32[4096]{0:T(1024)S(1)} %copy-done.6), kind=kOutput, calls=%fused_computation.147 | convolution fusion | flops 1881833472 | bytes 18301440 | tf_op jit(solution)/shard_map/dot_general | solution.py:158
  456.7 84.7 %all-gather.13.cloned.1.call-done = f32[1024,4096]{1,0:T(8,128)} async-done(((f32[128,4096]{1,0:T(8,128)}), f32[1024,4096]{1,0:T(8,128)}) %all-gather.13.cloned.1.call-update) | async-done | bytes 16777232 | tf_op jit(solution)/shard_map/all_gather | solution.py:158
  541.4 8.8 %reduce_sum.113 = f32[128,4096]{1,0:T(8,128)} reduce(f32[8,128,4096]{2,1,0:T(8,128)} %bitcast.297, f32[]{:T(128)} %constant.65.clone.1), dimensions={0}, to_apply=%region_23.24 | reduce | flops 3670016 | bytes 18874372 | tf_op jit(solution)/shard_map/reduce_sum | solution.py:157
  550.2 2.8 fusion.91
  (370 shorter events, 94.7 us)
Async XLA Ops:
  7.4 1.9 copy-start
  7.4 143.8 %all-reduce.3.cloned.1.call-start = ((), (), s32[]{:S(2)}) async-start(), calls=%async_computation | async-start | bytes 4194304 | tf_op jit(solution)/shard_map/psum | solution.py:147
  7.4 9.0 %copy-start.9 = (f32[64]{0:T(128)}, f32[64]{0:T(128)S(1)}, u32[]{:S(2)}) copy-start(f32[64]{0:T(128)S(1)} %multiply_power_fusion) | copy-start | bytes 772
  9.3 3.3 copy-start.14
  9.3 3.5 copy-start.2
  9.3 3.5 copy-start.11
  12.8 3.6 copy-start.7
  25.2 6.5 %copy-start.5 = (bf16[1,512,256]{2,1,0:T(8,128)(2,1)S(1)}, bf16[1,512,256]{2,1,0:T(8,128)(2,1)}, u32[]{:S(2)}) copy-start(bf16[1,512,256]{2,1,0:T(8,128)(2,1)} %param.24) | copy-start | bytes 786436
  81.5 72.6 %all-gather.7.cloned.1.call-start = ((), (), s32[]{:S(2)}) async-start(), calls=%async_computation.1 | async-start | bytes 7798784 | tf_op jit(solution)/shard_map/all_gather | solution.py:151
  82.0 138.9 %all-gather.9.cloned.1.call-start = ((), (), s32[]{:S(2)}) async-start(), calls=%async_computation.2 | async-start | bytes 7798784 | tf_op jit(solution)/shard_map/all_gather | solution.py:152
  82.6 71.4 %copy-start.6 = (f32[4096]{0:T(1024)S(1)}, f32[4096]{0:T(1024)}, u32[]{:S(2)}) copy-start(f32[4096]{0:T(1024)} %param.30) | copy-start | bytes 49156
  82.6 232.1 %all-gather.11.cloned.1.call-start = ((), (), s32[]{:S(2)}) async-start(), calls=%async_computation.4 | async-start | bytes 18874368 | tf_op jit(solution)/shard_map/all_gather | solution.py:158
  230.1 211.2 %all-reduce.5.cloned.1.call-start = ((), (), s32[]{:S(2)}) async-start(), calls=%async_computation.3 | async-start | bytes 4194304 | tf_op jit(solution)/shard_map/psum | solution.py:147
  323.5 3.5 copy-start.12
  326.0 1.0 copy-start.3
  327.0 0.7 copy-start.13
  327.7 3.3 copy-start.8
  327.7 3.3 copy-start.10
  331.0 1.0 copy-start.15
  374.9 66.4 %copy-start.4 = (bf16[128,4096]{1,0:T(8,128)(2,1)S(1)}, bf16[128,4096]{1,0:T(8,128)(2,1)}, u32[]{:S(2)}) copy-start(bf16[128,4096]{1,0:T(8,128)(2,1)} %copy-done.3) | copy-start | bytes 3145732
  374.9 166.5 %all-gather.13.cloned.1.call-start = ((), (), s32[]{:S(2)}) async-start(), calls=%async_computation.5 | async-start | bytes 18874368 | tf_op jit(solution)/shard_map/all_gather | solution.py:158
  541.4 11.6 %copy-start.1 = (bf16[4096,256]{1,0:T(8,128)(2,1)S(1)}, bf16[4096,256]{1,0:T(8,128)(2,1)}, u32[]{:S(2)}) copy-start(bf16[4096,256]{1,0:T(8,128)(2,1)} %param.28) | copy-start | bytes 6291460
Sparse Core Ops, SparseCore 0:
  81.6 69.5 all-reduce.2
  230.2 84.4 all-gather.10
  375.1 66.1 all-reduce.4
  456.9 84.4 all-gather.12
Sparse Core Ops, SparseCore 1:
  84.1 68.8 all-gather.6
  155.0 65.9 all-gather.8
